TPU v7x, 32 devices: a whole 2x2x4 slice. The times are simulated.
32 devices in a mesh: seq: 4 (over y, core), dp: 8 (over z, x).
Axes of the slice: x: 2, y: 2, z: 4, core: 2. Of those that a mesh axis runs over, the one named last changes fastest.
Arguments:
- tokens: bfloat16 [16, 1024, 1024], P('dp', 'seq'), may hold values from -6 to 6
- cotangent: bfloat16 [16, 1024, 1024], P('dp', 'seq'), may hold values from -6 to 6
- row_lengths: int32 [16], P('dp'), may hold values from 512 to 1024
- source_lengths: int32 [16], P('dp'), may hold values from 30 to 400
- first_gain: float32 [1024], replicated, may hold values from 0.1 to 1.9
- first_shift: float32 [1024], replicated, may hold values from -2 to 2
- attend_weight: bfloat16 [1024, 3072], replicated, may hold values from -0.25 to 0.25
- attend_bias: float32 [3072], replicated, may hold values from -2 to 2
- output_weight: bfloat16 [1024, 1024], replicated, may hold values from -0.75 to 0.75
- output_bias: float32 [1024], replicated, may hold values from -2 to 2
- second_gain: float32 [1024], replicated, may hold values from 0.1 to 1.9
- second_shift: float32 [1024], replicated, may hold values from -2 to 2
- expand_weight: bfloat16 [1024, 4096], replicated, may hold values from -0.1875 to 0.1875
- expand_bias: float32 [4096], replicated, may hold values from -2 to 2
- contract_weight: bfloat16 [4096, 1024], replicated, may hold values from -0.09375 to 0.09375
- contract_bias: float32 [1024], replicated, may hold values from -2 to 2
- prefix_table: bfloat16 [10, 1024], replicated, may hold values from -6 to 6
- lift_weight: bfloat16 [1024, 512], replicated, may hold values from -0.1875 to 0.1875
- lift_bias: float32 [512], replicated, may hold values from -2 to 2
- fan_weight: bfloat16 [512, 2048], replicated, may hold values from -0.375 to 0.375
- fan_bias: float32 [2048], replicated, may hold values from -2 to 2
Outputs:
- activations: bfloat16 [16, 1024, 1024], P('dp', 'seq')
- input_grad: float32 [16, 1024, 1024], P('dp', 'seq')
- grad_table: float32 [10, 1024], replicated
- grad_lift: float32 [1024, 512], replicated
- grad_liftbias: float32 [512], replicated
- grad_fan: float32 [512, 2048], replicated
- grad_fanbias: float32 [2048], replicated
All inputs are finite; a program needn't handle non-finite values.
Results may differ from a plain program's by a relative error of at most 0.025.
Values may be sent and summed in bfloat16 or wider, within the bound.
No kernel may reach another device: no remote copies, remote signals or barrier semaphores. Data moves between devices by JAX's collectives and lax.ppermute only.
A program may use at most 320 MiB of HBM per device.

v0:
```python
import jax
import jax.numpy as jnp
from jax import lax
from jax.sharding import PartitionSpec as P

D = 1024
HEADS = 16
HEAD_DIM = 64
PREFIX = 10
best_precision = lax.Precision.HIGHEST


def layer_norm(values, norm_gain, norm_shift):
    centred = values - jnp.mean(values, axis=-1, keepdims=True)
    variance = jnp.mean(centred * centred, axis=-1, keepdims=True)
    return centred * lax.rsqrt(variance + 1e-05) * norm_gain + norm_shift


def gelu_tanh(values):
    return jax.nn.gelu(values, approximate=True)


def block_forward(tokens, row_lengths, frozen, prefix_keyval, again):
    (
        first_gain,
        first_shift,
        attend_weight,
        attend_bias,
        output_weight,
        output_bias,
        second_gain,
        second_shift,
        expand_weight,
        expand_bias,
        contract_weight,
        contract_bias,
    ) = frozen
    row_count = tokens.shape[0]
    tok_count = tokens.shape[1]
    inputs = tokens.astype(jnp.float32)
    normed = layer_norm(inputs, first_gain, first_shift).astype(jnp.bfloat16)
    project = jnp.dot(normed, attend_weight, preferred_element_type=jnp.float32) + attend_bias
    queries = project[..., :D].astype(jnp.bfloat16).reshape(row_count, tok_count, HEADS, HEAD_DIM)
    local_keyval = project[..., D:].astype(jnp.bfloat16)
    if again:
        row_keyval = lax.all_gather(local_keyval, "seq", axis=1, tiled=True)
    else:
        row_keyval = lax.all_gather(local_keyval, "seq", axis=1, tiled=True)
    seq_total = row_keyval.shape[1]
    row_keys = row_keyval[..., :D].reshape(row_count, seq_total, HEADS, HEAD_DIM)
    row_values = row_keyval[..., D:].reshape(row_count, seq_total, HEADS, HEAD_DIM)
    prefix_keys = prefix_keyval[:, :D].reshape(PREFIX, HEADS, HEAD_DIM)
    prefix_values = prefix_keyval[:, D:].reshape(PREFIX, HEADS, HEAD_DIM)
    scores = (
        jnp.einsum("rqhd,rkhd->rhqk", queries, row_keys, preferred_element_type=jnp.float32) * 0.125
    )
    prefix_scores = (
        jnp.einsum("rqhd,phd->rhqp", queries, prefix_keys, preferred_element_type=jnp.float32)
        * 0.125
    )
    query_places = lax.axis_index("seq") * tok_count + jnp.arange(tok_count)
    key_places = jnp.arange(seq_total)
    visible = (key_places[None, None, :] <= query_places[None, :, None]) & (
        key_places[None, None, :] < row_lengths[:, None, None]
    )
    scores = jnp.where(visible[:, None], scores, -jnp.inf)
    highest = jnp.maximum(
        jnp.max(scores, axis=-1, keepdims=True), jnp.max(prefix_scores, axis=-1, keepdims=True)
    )
    denominator = jnp.sum(jnp.exp(scores - highest), axis=-1, keepdims=True) + jnp.sum(
        jnp.exp(prefix_scores - highest), axis=-1, keepdims=True
    )
    log_total = highest + jnp.log(denominator)
    weights = jnp.exp(scores - log_total)
    prefix_weights = jnp.exp(prefix_scores - log_total)
    rounded = weights.astype(jnp.bfloat16)
    prefix_rounded = prefix_weights.astype(jnp.bfloat16)
    attended = jnp.einsum(
        "rhqk,rkhd->rqhd", rounded, row_values, preferred_element_type=jnp.float32
    )
    attended = attended + jnp.einsum(
        "rhqp,phd->rqhd", prefix_rounded, prefix_values, preferred_element_type=jnp.float32
    )
    mixed_heads = attended.reshape(row_count, tok_count, D).astype(jnp.bfloat16)
    residual = (
        inputs
        + jnp.dot(mixed_heads, output_weight, preferred_element_type=jnp.float32)
        + output_bias
    )
    normed_two = layer_norm(residual, second_gain, second_shift).astype(jnp.bfloat16)
    expanded = jnp.dot(normed_two, expand_weight, preferred_element_type=jnp.float32) + expand_bias
    activated = gelu_tanh(expanded).astype(jnp.bfloat16)
    result = (
        residual
        + jnp.dot(activated, contract_weight, preferred_element_type=jnp.float32)
        + contract_bias
    )
    return (
        inputs,
        queries,
        row_keys,
        row_values,
        prefix_keys,
        prefix_values,
        weights,
        prefix_weights,
        rounded,
        prefix_rounded,
        residual,
        expanded,
        result,
        log_total,
    )


def prefix_grads(prefix_grad, prefix_table, lift_weight, fan_weight, lifted, lifted_low):
    grad_fanbias = jnp.sum(prefix_grad, axis=0)
    grad_fan = jnp.dot(lifted_low.astype(jnp.float32).T, prefix_grad, precision=best_precision)
    grad_lifted = jnp.dot(
        prefix_grad, fan_weight.astype(jnp.float32).T, precision=best_precision
    ) * (1.0 - lifted * lifted)
    grad_liftbias = jnp.sum(grad_lifted, axis=0)
    grad_lift = jnp.dot(prefix_table.astype(jnp.float32).T, grad_lifted, precision=best_precision)
    grad_table = jnp.dot(grad_lifted, lift_weight.astype(jnp.float32).T, precision=best_precision)
    return (grad_table, grad_lift, grad_liftbias, grad_fan, grad_fanbias)


def per_device(
    tokens,
    cotangent,
    row_lengths,
    source_lengths,
    first_gain,
    first_shift,
    attend_weight,
    attend_bias,
    output_weight,
    output_bias,
    second_gain,
    second_shift,
    expand_weight,
    expand_bias,
    contract_weight,
    contract_bias,
    prefix_table,
    lift_weight,
    lift_bias,
    fan_weight,
    fan_bias,
):
    frozen = (
        first_gain,
        first_shift,
        attend_weight,
        attend_bias,
        output_weight,
        output_bias,
        second_gain,
        second_shift,
        expand_weight,
        expand_bias,
        contract_weight,
        contract_bias,
    )
    lifted = jnp.tanh(
        jnp.dot(prefix_table, lift_weight, preferred_element_type=jnp.float32) + lift_bias
    )
    lifted_low = lifted.astype(jnp.bfloat16)
    prefix_keyval = (
        jnp.dot(lifted_low, fan_weight, preferred_element_type=jnp.float32) + fan_bias
    ).astype(jnp.bfloat16)
    state = block_forward(tokens, row_lengths, frozen, prefix_keyval, False)
    activations = state[12].astype(jnp.bfloat16)
    again_tokens = lax.optimization_barrier((tokens, activations))[0]
    state = block_forward(again_tokens, row_lengths, frozen, prefix_keyval, True)
    (
        inputs,
        queries,
        row_keys,
        row_values,
        prefix_keys,
        prefix_values,
        weights,
        prefix_weights,
        rounded,
        prefix_rounded,
        residual,
        expanded,
        result,
        log_total,
    ) = state
    row_count = tokens.shape[0]
    tok_count = tokens.shape[1]
    places = lax.axis_index("seq") * tok_count + jnp.arange(tok_count)
    target = (places[None, :] >= source_lengths[:, None]) & (places[None, :] < row_lengths[:, None])
    grad_out = jnp.where(target[..., None], cotangent, jnp.zeros_like(cotangent))
    grad_hidden = jnp.einsum(
        "rcd,fd->rcf", grad_out, contract_weight, preferred_element_type=jnp.float32
    )
    _, gelu_back = jax.vjp(gelu_tanh, expanded)
    grad_expand = gelu_back(grad_hidden)[0].astype(jnp.bfloat16)
    grad_normed = jnp.einsum(
        "rcf,df->rcd", grad_expand, expand_weight, preferred_element_type=jnp.float32
    )
    _, second_back = jax.vjp(lambda values: layer_norm(values, second_gain, second_shift), residual)
    grad_residual = grad_out.astype(jnp.float32) + second_back(grad_normed)[0]
    grad_mixed = jnp.einsum(
        "rcd,ed->rce",
        grad_residual.astype(jnp.bfloat16),
        output_weight,
        preferred_element_type=jnp.float32,
    )
    grad_heads = grad_mixed.astype(jnp.bfloat16).reshape(row_count, tok_count, HEADS, HEAD_DIM)
    grad_weights = jnp.einsum(
        "rqhd,rkhd->rhqk", grad_heads, row_values, preferred_element_type=jnp.float32
    )
    grad_preweights = jnp.einsum(
        "rqhd,phd->rhqp", grad_heads, prefix_values, preferred_element_type=jnp.float32
    )
    inner_sum = jnp.sum(weights * grad_weights, axis=-1, keepdims=True) + jnp.sum(
        prefix_weights * grad_preweights, axis=-1, keepdims=True
    )
    grad_scores = (weights * (grad_weights - inner_sum)).astype(jnp.bfloat16)
    grad_prescores = (prefix_weights * (grad_preweights - inner_sum)).astype(jnp.bfloat16)
    grad_queries = jnp.einsum(
        "rhqk,rkhd->rqhd", grad_scores, row_keys, preferred_element_type=jnp.float32
    )
    grad_queries = (
        grad_queries
        + jnp.einsum(
            "rhqp,phd->rqhd", grad_prescores, prefix_keys, preferred_element_type=jnp.float32
        )
    ) * 0.125
    grad_keys = (
        jnp.einsum("rhqk,rqhd->krhd", grad_scores, queries, preferred_element_type=jnp.float32)
        * 0.125
    )
    grad_values = jnp.einsum(
        "rhqk,rqhd->krhd", rounded, grad_heads, preferred_element_type=jnp.float32
    )
    owned = lax.psum_scatter(
        jnp.concatenate(
            [
                grad_keys.reshape(tok_count * lax.axis_size("seq"), row_count, D),
                grad_values.reshape(tok_count * lax.axis_size("seq"), row_count, D),
            ],
            axis=-1,
        ).astype(jnp.bfloat16),
        "seq",
        scatter_dimension=0,
        tiled=True,
    ).astype(jnp.float32)
    grad_owned = jnp.transpose(owned, (1, 0, 2)).astype(jnp.bfloat16)
    grad_prekeys = (
        jnp.einsum("rhqp,rqhd->phd", grad_prescores, queries, preferred_element_type=jnp.float32)
        * 0.125
    )
    grad_prevalues = jnp.einsum(
        "rhqp,rqhd->phd", prefix_rounded, grad_heads, preferred_element_type=jnp.float32
    )
    prefix_grad = jnp.concatenate(
        [grad_prekeys.reshape(PREFIX, D), grad_prevalues.reshape(PREFIX, D)], axis=-1
    )
    grad_project = jnp.concatenate(
        [grad_queries.reshape(row_count, tok_count, D).astype(jnp.bfloat16), grad_owned], axis=-1
    )
    grad_first = jnp.einsum(
        "rcf,df->rcd", grad_project, attend_weight, preferred_element_type=jnp.float32
    )
    _, first_back = jax.vjp(lambda values: layer_norm(values, first_gain, first_shift), inputs)
    input_grad = grad_residual + first_back(grad_first)[0]
    grad_table, grad_lift, grad_liftbias, grad_fan, grad_fanbias = prefix_grads(
        prefix_grad, prefix_table, lift_weight, fan_weight, lifted, lifted_low
    )
    grad_table, grad_lift, grad_liftbias, grad_fan, grad_fanbias = lax.psum(
        (grad_table, grad_lift, grad_liftbias, grad_fan, grad_fanbias), ("seq", "dp")
    )
    return (activations, input_grad, grad_table, grad_lift, grad_liftbias, grad_fan, grad_fanbias)


def solution(mesh):
    return jax.shard_map(
        per_device,
        mesh=mesh,
        in_specs=(
            P("dp", "seq", None),
            P("dp", "seq", None),
            P("dp"),
            P("dp"),
            P(),
            P(),
            P(),
            P(),
            P(),
            P(),
            P(),
            P(),
            P(),
            P(),
            P(),
            P(),
            P(),
            P(),
            P(),
            P(),
            P(),
        ),
        out_specs=(P("dp", "seq", None), P("dp", "seq", None), P(), P(), P(), P(), P()),
        check_vma=False,
    )
```

profile of v0, /device:TPU:0, one launch (start us, length us, event | category | flops | bytes accessed | tf_op | source)
XLA Modules:
  0.0 668.7 jit_solution(5564932534469927278)
XLA Ops:
  10.5 6.6 add_convert_fusion.1
  20.8 2.3 slice.48
  28.7 52.7 %all-gather.3.cloned.1.call-done = bf16[2,1024,2048]{2,1,0:T(8,128)(2,1)} async-done(((bf16[2,256,2048]{2,1,0:T(8,128)(2,1)}), bf16[2,1024,2048]{2,1,0:T(8,128)(2,1)}) %all-gather.3.cloned.1.call-update) | async-done | bytes 8388624 | tf_op jit(solution)/shard_map/all_gather | solution.py:48
  81.4 6.0 fusion.174
  87.4 6.2 copy.171
  93.6 6.2 copy.173
  99.8 15.9 %fusion = (f32[2,16,256]{2,1,0:T(8,128)S(1)}, f32[2,16,256,1024]{3,2,1,0:T(8,128)}) fusion(pred[2,256,1024]{2,1,0:T(8,128)(4,1)S(1)} %broadcast_and_fusion, bf16[2,256,16,64]{1,3,2,0:T(8,128)(2,1)} %bitcast.197, bf16[2,1024,16,64]{1,3,2,0:T(8,128)(2,1)} %bitcast.195), kind=kOutput, calls=%fused_computation.8 | convolution fusion | flops 1098899456 | bytes 39354368 | tf_op jit(solution)/shard_map/rqhd,rkhd->rhqk/dot_general | solution.py:55
  116.0 14.9 %exponential_reduce_fusion.1 = f32[2,16,256]{2,1,0:T(8,128)S(1)} fusion(f32[2,16,256,1024]{3,2,1,0:T(8,128)} %get-tuple-element.60, f32[2,16,256]{2,1,0:T(8,128)S(1)} %max.22, pred[2,256,1024]{2,1,0:T(8,128)(4,1)S(1)} %broadcast_and_fusion), kind=kLoop, calls=%fused_computation.6 | loop fusion | flops 33546240 | bytes 34144256 | tf_op jit(solution)/shard_map/reduce_sum | solution.py:70
  132.9 17.5 %fusion.74 = bf16[2,256,16,64]{1,3,2,0:T(8,128)(2,1)} fusion(f32[16,64,2,256]{3,1,0,2:T(8,128)} %fusion.137, bf16[2,1024,16,64]{1,3,2,0:T(8,128)(2,1)} %bitcast.198, f32[2,16,256,1024]{3,2,1,0:T(8,128)} %get-tuple-element.60, f32[2,16,256]{2,1,0:T(8,128)S(1)} %log_add_fusion.1, pred[2,256,1024]{2,1,0:T(8,128)(4,1)} %copy-done.2), kind=kOutput, calls=%fused_computation.94 | convolution fusion | flops 1108344832 | bytes 41451520 | tf_op jit(solution)/shard_map/rhqk,rkhd->rqhd/dot_general | solution.py:78
  150.5 2.7 fusion.176
  153.7 10.4 %fusion.19 = bf16[2,256,4096]{2,1,0:T(8,128)(2,1)S(1)} fusion(bf16[1024,4096]{1,0:T(8,128)(2,1)} %param.33, f32[4096]{0:T(1024)S(1)} %copy-done.45, f32[2,256,1024]{2,1,0:T(8,128)S(1)} %get-tuple-element.62, f32[1024]{0:T(1024)S(1)} %copy-done.49, f32[1024]{0:T(1024)S(1)} %copy-done.38, f32[2,256]{1,0:T(2,128)S(1)} %add_rsqrt_fusion, ...), kind=kOutput, calls=%fused_computation.30 | convolution fusion | flops 4318560256 | bytes 14708736 | tf_op jit(solution)/shard_map/dot_general | solution.py:91
  164.2 5.5 add_convert_fusion.3
  170.5 4.0 add_convert_fusion
  177.8 12.7 %fusion.20 = f32[2,256,4096]{2,1,0:T(8,128)} fusion(bf16[4096,1024]{1,0:T(8,128)(2,1)} %param.35, bf16[2,256,1024]{2,1,0:T(8,128)(2,1)} %param.22, pred[2,256]{1,0:T(4,128)(4,1)S(1)} %compare_and_fusion), kind=kOutput, calls=%fused_computation.32 | convolution fusion | flops 4295491584 | bytes 17826304 | tf_op jit(solution)/shard_map/rcd,fd->rcf/dot_general | solution.py:197
  190.6 2.3 slice.54
  192.9 2.5 copy.185
  197.0 39.1 %all-gather.5.cloned.1.call-done = bf16[2,1024,2048]{2,1,0:T(8,128)(2,1)} async-done(((bf16[2,256,2048]{2,1,0:T(8,128)(2,1)}), bf16[2,1024,2048]{2,1,0:T(8,128)(2,1)}) %all-gather.5.cloned.1.call-update) | async-done | bytes 8388624 | tf_op jit(solution)/shard_map/all_gather | solution.py:46
  236.2 6.0 fusion.173
  242.2 6.2 copy.186
  248.4 6.2 copy.184
  254.6 15.9 %fusion.1 = (f32[2,16,256]{2,1,0:T(8,128)S(1)}, f32[2,16,256,1024]{3,2,1,0:T(8,128)}) fusion(pred[2,256,1024]{2,1,0:T(8,128)(4,1)} %copy-done.2, bf16[2,256,16,64]{1,3,2,0:T(8,128)(2,1)} %bitcast.185, bf16[2,1024,16,64]{1,3,2,0:T(8,128)(2,1)} %bitcast.182), kind=kOutput, calls=%fused_computation.9 | convolution fusion | flops 1098899456 | bytes 39354368 | tf_op jit(solution)/shard_map/rqhd,rkhd->rhqk/dot_general | solution.py:55
  270.5 14.9 %exponential_reduce_fusion = f32[2,16,256]{2,1,0:T(8,128)S(1)} fusion(f32[2,16,256,1024]{3,2,1,0:T(8,128)} %get-tuple-element.64, f32[2,16,256]{2,1,0:T(8,128)S(1)} %max.23, pred[2,256,1024]{2,1,0:T(8,128)(4,1)S(1)} %copy-done.3), kind=kLoop, calls=%fused_computation.3 | loop fusion | flops 33546240 | bytes 34144256 | tf_op jit(solution)/shard_map/reduce_sum | solution.py:70
  286.2 17.0 %fusion.141 = f32[2,16,64,256]{3,2,1,0:T(8,128)} fusion(bf16[2,1024,16,64]{1,3,2,0:T(8,128)(2,1)} %bitcast.188, f32[2,16,256,1024]{3,2,1,0:T(8,128)} %get-tuple-element.64, f32[2,16,256]{2,1,0:T(8,128)S(1)} %log_add_fusion, pred[2,256,1024]{2,1,0:T(8,128)(4,1)} %copy-done.2), kind=kOutput, calls=%fused_computation.169 | convolution fusion | flops 1107296256 | bytes 40402944 | tf_op jit(solution)/shard_map/rhqk,rkhd->rqhd/dot_general | solution.py:78
  303.2 2.2 fusion.67
  309.0 23.9 %multiply_reduce_fusion.1 = (f32[2,256]{1,0:T(2,128)}, f32[2,256,1024]{2,1,0:T(8,128)}) fusion(f32[2,256,1024]{2,1,0:T(8,128)} %copy-done.4, f32[2,256]{1,0:T(2,128)S(1)} %broadcast_multiply_fusion, f32[1024]{0:T(1024)} %param.31, bf16[1024,4096]{1,0:T(8,128)(2,1)} %param.33, f32[2,256,4096]{2,1,0:T(8,128)} %fusion.20, f32[4096]{0:T(1024)} %param.34, ...), kind=kOutput, calls=%fused_computation.97 | convolution fusion | flops 8638693376 | bytes 21002240 | tf_op jit(solution)/shard_map/rcf,df->rcd/dot_general | solution.py:202
  333.7 2.9 fusion.172
  337.9 2.4 fusion.77
  340.3 2.2 copy.197
  344.1 27.3 %multiply_reduce_fusion = (f32[2,16,256]{2,1,0:T(8,128)}, f32[2,16,256,1024]{3,2,1,0:T(8,128)}) fusion(f32[2,16,256,1024]{3,2,1,0:T(8,128)} %get-tuple-element.64, f32[2,16,256]{2,1,0:T(8,128)S(1)} %log_add_fusion, pred[2,256,1024]{2,1,0:T(8,128)(4,1)} %copy-done.2, bf16[2,256,16,64]{1,3,2,0:T(8,128)(2,1)} %bitcast.192, bf16[2,1024,16,64]{1,3,2,0:T(8,128)(2,1)} %bitcast.189), kind=kOutput, calls=%fused_computation.1 | convolution fusion | flops 1115676672 | bytes 72941568 | tf_op jit(solution)/shard_map/rqhd,rkhd->rhqk/dot_general | solution.py:214
  380.2 3.3 fusion.180
  383.6 3.8 fusion.152
  387.4 28.0 %multiply_convert_fusion = bf16[2,16,256,1024]{3,2,1,0:T(8,128)(2,1)} fusion(f32[2,16,256,1024]{3,2,1,0:T(8,128)} %get-tuple-element.70, f32[2,16,256,1024]{3,2,1,0:T(8,128)} %get-tuple-element.64, f32[2,16,256]{2,1,0:T(8,128)S(1)} %copy-done.23, f32[2,16,256]{2,1,0:T(8,128)S(1)} %log_add_fusion, pred[2,256,1024]{2,1,0:T(8,128)(4,1)} %copy-done.2), kind=kLoop, calls=%fused_computation | loop fusion | flops 50331648 | bytes 84475904 | tf_op jit(solution)/shard_map/convert_element_type | solution.py:223
  415.3 2.3 convolution_bitcast_fusion
  417.8 18.1 %convolution_convert_fusion = bf16[2,16,64,1024]{3,2,1,0:T(8,128)(2,1)} fusion(bf16[2,256,16,64]{1,3,2,0:T(8,128)(2,1)} %bitcast.194, f32[2,16,256,1024]{3,2,1,0:T(8,128)} %get-tuple-element.64, f32[2,16,256]{2,1,0:T(8,128)S(1)} %log_add_fusion, pred[2,256,1024]{2,1,0:T(8,128)(4,1)} %copy-done.2), kind=kOutput, calls=%fused_computation.66 | convolution fusion | flops 1109393408 | bytes 39354368 | tf_op jit(solution)/shard_map/rhqk,rqhd->krhd/dot_general | solution.py:238
  435.8 6.3 copy.206
  442.2 11.3 %multiply_convert_fusion.1 = bf16[2,16,64,1024]{3,2,1,0:T(8,128)(2,1)} fusion(bf16[2,256,16,64]{1,3,2,0:T(8,128)(2,1)} %bitcast.187, bf16[2,16,256,1024]{3,2,1,0:T(8,128)(2,1)} %multiply_convert_fusion), kind=kOutput, calls=%fused_computation.42 | convolution fusion | flops 1077936128 | bytes 22020096 | tf_op jit(solution)/shard_map/rhqk,rqhd->krhd/dot_general | solution.py:235
  453.5 6.5 copy.205
  460.0 8.5 %pad_maximum_fusion = bf16[1024,2,2048]{2,0,1:T(8,128)(2,1)} fusion(bf16[1024,2,1024]{2,0,1:T(8,128)(2,1)} %copy.206, bf16[1024,2,1024]{2,0,1:T(8,128)(2,1)} %copy.205), kind=kLoop, calls=%fused_computation.31 | loop fusion | flops 16777216 | bytes 16777216 | tf_op jit(solution)/shard_map/concatenate | solution.py:242
  468.5 13.8 %fusion.181 = f32[2,16,64,256]{3,2,1,0:T(8,128)} fusion(bf16[2,1024,16,64]{1,3,2,0:T(8,128)(2,1)} %bitcast.183, bf16[2,16,256,1024]{3,2,1,0:T(8,128)(2,1)} %multiply_convert_fusion), kind=kOutput, calls=%fused_computation.225 | convolution fusion | flops 1073741824 | bytes 23068672 | tf_op jit(solution)/shard_map/rhqk,rkhd->rqhd/dot_general | solution.py:225
  482.4 3.1 fusion.66
  485.4 2.3 copy.207
  487.8 2.1 fusion.182
  489.9 40.9 %all-reduce = (f32[10,1024]{1,0:T(8,128)}, f32[512]{0:T(512)}, f32[2048]{0:T(1024)}) all-reduce(f32[10,1024]{1,0:T(8,128)S(1)} %fusion.182, f32[512]{0:T(512)S(1)} %get-tuple-element.73, f32[2048]{0:T(1024)S(1)} %reduce_sum.231), channel_id=1, replica_groups=mesh['seq'=4,'dp'=8] {'seq','dp'}, use_global_device_ids=true, to_apply=%region_23.24 | all-reduce | flops 12800 | bytes 102400 | tf_op jit(solution)/shard_map/psum | solution.py:275
  530.8 43.5 %all-reduce.4.cloned.1.call-done = (f32[1024,512]{0,1:T(8,128)}, f32[512,2048]{1,0:T(8,128)}) async-done(((f32[1024,512]{0,1:T(8,128)}, f32[512,2048]{1,0:T(8,128)}), (f32[1024,512]{0,1:T(8,128)}, f32[512,2048]{1,0:T(8,128)})) %all-reduce.4.cloned.1.call-update) | async-done | bytes 6291472 | tf_op jit(solution)/shard_map/psum | solution.py:275
  574.3 2.9 copy.212
  577.1 71.4 %reduce-scatter.2.cloned.1.call-done = bf16[256,2,2048]{2,0,1:T(8,128)(2,1)} async-done(((bf16[1024,2,2048]{2,0,1:T(8,128)(2,1)}), bf16[256,2,2048]{2,0,1:T(8,128)(2,1)}) %reduce-scatter.2.cloned.1.call-update) | async-done | bytes 2097168 | tf_op jit(solution)/shard_map/reduce_scatter | solution.py:241
  648.6 6.7 %fusion.63 = (f32[2,256]{1,0:T(2,128)S(1)}, f32[2,256,1024]{2,1,0:T(8,128)S(1)}) fusion(bf16[2,256,1024]{2,1,0:T(8,128)(2,1)S(1)} %copy-done.1, f32[2,256]{1,0:T(2,128)S(1)} %copy-done.30, f32[1024]{0:T(1024)S(1)} %copy-done.36, bf16[1024,3072]{1,0:T(8,128)(2,1)} %param.27, bf16[2,256,2048]{2,1,0:T(8,128)(2,1)} %bitcast.210, bf16[2,256,1024]{2,1,0:T(8,128)(2,1)} %copy.207), kind=kOutput, calls=%fused_computation.80 | convolution fusion | flops 3230137856 | bytes 12591104 | tf_op jit(solution)/shard_map/rcf,df->rcd/dot_general | solution.py:267
  656.9 2.1 add_add_fusion.2
  (178 shorter events, 42.4 us)
Async XLA Ops:
  7.2 143.2 %copy-start = (bf16[1024,1024]{1,0:T(8,128)(2,1)S(1)}, bf16[1024,1024]{1,0:T(8,128)(2,1)}, u32[]{:S(2)}) copy-start(bf16[1024,1024]{1,0:T(8,128)(2,1)} %param.29) | copy-start | bytes 6291460
  7.2 74.2 %all-gather.3.cloned.1.call-start = ((), (), s32[]{:S(2)}) async-start(), calls=%async_computation.1 | async-start | bytes 10485760 | tf_op jit(solution)/shard_map/all_gather | solution.py:48
  18.7 4.3 copy-start.11
  18.7 4.3 copy-start.26
  18.7 4.3 copy-start.42
  18.7 4.6 copy-start.37
  20.3 215.9 %all-gather.5.cloned.1.call-start = ((), (), s32[]{:S(2)}) async-start(), calls=%async_computation.2 | async-start | bytes 10485760 | tf_op jit(solution)/shard_map/all_gather | solution.py:46
  23.0 4.5 copy-start.43
  23.3 2.0 copy-start.20
  25.6 169.8 %copy-start.16 = (bf16[10,16,64]{2,1,0:T(8,128)(2,1)}, bf16[10,16,64]{2,1,0:T(8,128)(2,1)S(1)}, u32[]{:S(2)}) copy-start(bf16[10,16,64]{2,1,0:T(8,128)(2,1)S(1)} %reshape.304) | copy-start | bytes 61444
  28.7 87.3 %copy-start.2 = (pred[2,256,1024]{2,1,0:T(8,128)(4,1)}, pred[2,256,1024]{2,1,0:T(8,128)(4,1)S(1)}, u32[]{:S(2)}) copy-start(pred[2,256,1024]{2,1,0:T(8,128)(4,1)S(1)} %broadcast_and_fusion) | copy-start | bytes 1572868
  99.8 15.9 %copy-start.7 = (f32[16,10,2,256]{3,1,2,0:T(8,128)S(1)}, f32[16,10,2,256]{3,1,2,0:T(8,128)}, u32[]{:S(2)}) copy-start(f32[16,10,2,256]{3,1,2,0:T(8,128)} %copy-done.6) | copy-start | bytes 983044
  132.9 17.5 %copy-start.1 = (bf16[2,256,1024]{2,1,0:T(8,128)(2,1)S(1)}, bf16[2,256,1024]{2,1,0:T(8,128)(2,1)}, u32[]{:S(2)}) copy-start(bf16[2,256,1024]{2,1,0:T(8,128)(2,1)} %param.21) | copy-start | bytes 3145732
  132.9 17.5 %copy-start.28 = (f32[1024]{0:T(1024)S(1)}, f32[1024]{0:T(1024)}, u32[]{:S(2)}) copy-start(f32[1024]{0:T(1024)} %param.30) | copy-start | bytes 12292
  150.4 3.2 copy-start.38
  150.5 3.2 copy-start.45
  150.5 3.2 copy-start.49
  150.5 13.6 %slice-start = ((s8[8388608]{0:T(1024)(128)(4,1)}), s8[4194304]{0:T(1024)(128)(4,1)S(1)}, s32[]{:S(2)}) async-start(s8[8388608]{0:T(1024)(128)(4,1)} %bitcast.206), calls=%async_computation.5 | async-start | bytes 8388608
  150.5 19.9 %slice-start.2 = ((s8[6291456]{0:T(1024)(128)(4,1)}), s8[4194304]{0:T(1024)(128)(4,1)S(1)}, s32[]{:S(2)}) async-start(s8[6291456]{0:T(1024)(128)(4,1)} %bitcast.208), calls=%async_computation.7 | async-start | bytes 8388608
  153.6 10.5 %slice-start.1 = ((s8[8388608]{0:T(1024)(128)(4,1)}), s8[4194304]{0:T(1024)(128)(4,1)S(1)}, s32[]{:S(2)}) async-start(s8[8388608]{0:T(1024)(128)(4,1)} %bitcast.206), calls=%async_computation.6 | async-start | bytes 8388608
  153.7 10.5 %copy-start.47 = (f32[1024]{0:T(1024)S(1)}, f32[1024]{0:T(1024)}, u32[]{:S(2)}) copy-start(f32[1024]{0:T(1024)} %param.36) | copy-start | bytes 12292
  153.7 16.7 %slice-start.3 = ((s8[6291456]{0:T(1024)(128)(4,1)}), s8[2097152]{0:T(1024)(128)(4,1)S(1)}, s32[]{:S(2)}) async-start(s8[6291456]{0:T(1024)(128)(4,1)} %bitcast.208), calls=%async_computation.8 | async-start | bytes 4194304
  164.2 6.3 copy-start.35
  164.2 6.3 copy-start.46
  164.2 6.2 copy-start.48
  170.0 4.5 copy-start.29
  170.4 4.1 copy-start.31
  170.5 4.0 copy-start.33
  177.7 396.6 %all-reduce.4.cloned.1.call-start = ((), (), s32[]{:S(2)}) async-start(), calls=%async_computation.4 | async-start | bytes 12582912 | tf_op jit(solution)/shard_map/psum | solution.py:275
  177.8 12.8 %copy-start.39 = (pred[2,256]{1,0:T(4,128)(4,1)}, pred[2,256]{1,0:T(4,128)(4,1)S(1)}, u32[]{:S(2)}) copy-start(pred[2,256]{1,0:T(4,128)(4,1)S(1)} %compare_and_fusion) | copy-start | bytes 1540
  254.6 16.0 %copy-start.3 = (pred[2,256,1024]{2,1,0:T(8,128)(4,1)S(1)}, pred[2,256,1024]{2,1,0:T(8,128)(4,1)}, u32[]{:S(2)}) copy-start(pred[2,256,1024]{2,1,0:T(8,128)(4,1)} %copy-done.2) | copy-start | bytes 1572868
  332.9 5.0 copy-start.18
  332.9 5.0 copy-start.40
  375.1 8.4 %copy-start.21 = (f32[10,512]{1,0:T(8,128)S(1)}, f32[10,512]{1,0:T(8,128)}, u32[]{:S(2)}) copy-start(f32[10,512]{1,0:T(8,128)} %copy-done.20) | copy-start | bytes 61444
  377.6 9.8 %copy-start.23 = (f32[2,16,256]{2,1,0:T(8,128)S(1)}, f32[2,16,256]{2,1,0:T(8,128)}, u32[]{:S(2)}) copy-start(f32[2,16,256]{2,1,0:T(8,128)} %copy-done.22) | copy-start | bytes 98308
  383.6 31.8 %copy-start.24 = (f32[10,512]{1,0:T(8,128)}, f32[10,512]{1,0:T(8,128)S(1)}, u32[]{:S(2)}) copy-start(f32[10,512]{1,0:T(8,128)S(1)} %get-tuple-element.74) | copy-start | bytes 61444
  387.4 28.0 %copy-start.27 = (bf16[10,1024]{1,0:T(8,128)(2,1)S(1)}, bf16[10,1024]{1,0:T(8,128)(2,1)}, u32[]{:S(2)}) copy-start(bf16[10,1024]{1,0:T(8,128)(2,1)} %param.37) | copy-start | bytes 61444
  417.7 230.9 %reduce-scatter.2.cloned.1.call-start = ((), (), s32[]{:S(2)}) async-start(), calls=%async_computation.3 | async-start | bytes 10485760 | tf_op jit(solution)/shard_map/reduce_scatter | solution.py:241
  468.5 13.8 %copy-start.15 = (bf16[2,16,256,10]{2,1,3,0:T(8,128)(2,1)S(1)}, bf16[2,16,256,10]{2,1,3,0:T(8,128)(2,1)}, u32[]{:S(2)}) copy-start(bf16[2,16,256,10]{2,1,3,0:T(8,128)(2,1)} %copy-done.14) | copy-start | bytes 491524
  468.5 13.8 %copy-start.17 = (bf16[10,16,64]{2,1,0:T(8,128)(2,1)S(1)}, bf16[10,16,64]{2,1,0:T(8,128)(2,1)}, u32[]{:S(2)}) copy-start(bf16[10,16,64]{2,1,0:T(8,128)(2,1)} %copy-done.16) | copy-start | bytes 61444
  482.4 5.4 copy-start.25
  485.4 163.1 %copy-start.30 = (f32[2,256]{1,0:T(2,128)S(1)}, f32[2,256]{1,0:T(2,128)}, u32[]{:S(2)}) copy-start(f32[2,256]{1,0:T(2,128)} %copy-done.29) | copy-start | bytes 6148
  485.4 163.1 %copy-start.36 = (f32[1024]{0:T(1024)S(1)}, f32[1024]{0:T(1024)}, u32[]{:S(2)}) copy-start(f32[1024]{0:T(1024)} %param.25) | copy-start | bytes 12292
  648.6 6.8 %copy-start.32 = (f32[2,256]{1,0:T(2,128)S(1)}, f32[2,256]{1,0:T(2,128)}, u32[]{:S(2)}) copy-start(f32[2,256]{1,0:T(2,128)} %copy-done.31) | copy-start | bytes 6148
  648.6 6.8 %copy-start.34 = (f32[2,256]{1,0:T(2,128)S(1)}, f32[2,256]{1,0:T(2,128)}, u32[]{:S(2)}) copy-start(f32[2,256]{1,0:T(2,128)} %copy-done.33) | copy-start | bytes 6148
  648.6 7.5 %copy-start.19 = (bf16[2,256,1024]{2,1,0:T(8,128)(2,1)S(1)}, bf16[2,256,1024]{2,1,0:T(8,128)(2,1)}, u32[]{:S(2)}) copy-start(bf16[2,256,1024]{2,1,0:T(8,128)(2,1)} %param.22) | copy-start | bytes 3145732
  648.6 7.5 %copy-start.41 = (pred[2,256]{1,0:T(4,128)(4,1)S(1)}, pred[2,256]{1,0:T(4,128)(4,1)}, u32[]{:S(2)}) copy-start(pred[2,256]{1,0:T(4,128)(4,1)} %copy-done.39) | copy-start | bytes 1540
  656.9 2.9 copy-start.10
  (10 other events, 12.3 us)
Sparse Core Ops, SparseCore 0:
  20.4 60.9 all-gather.2
  177.8 58.2 all-gather.4
  417.8 156.4 all-reduce.3
  576.9 71.6 reduce-scatter.1
where the time goes:
time: 674 us; the launch traced here: 669 us
  matrix products  241 us (36%)
  waiting for transfers between devices  207 us (31%)
  local copies, waits for them, and re-layouts  83.7 us (12%)
  other arithmetic  81.4 us (12%)
  blocking collectives  40.9 us (6%)
  between operations  14.8 us (2%)
    all_gather x2, waiting for transfers between devices, block_forward(): row_keyval = lax.all_gather(local_keyval, 'seq', axis=1, tiled=True)  91.8 us
    reduce_scatter x1, waiting for transfers between devices, per_device(): lax.psum_scatter(jnp.concatenate([grad_keys.reshape(tok_count * lax.axis_...  71.4 us
    psum x1, waiting for transfers between devices, per_device(): lax.psum((grad_table, grad_lift, grad_liftbias, grad_fan, grad_fanbias),...  43.5 us
    psum x1, blocking collectives, per_device(): lax.psum((grad_table, grad_lift, grad_liftbias, grad_fan, grad_fanbias),...  40.9 us
    dot_general x2, matrix products, block_forward(): jnp.einsum('rhqk,rkhd->rqhd', rounded, row_values, preferred_element_type...  34.5 us
    dot_general x2, matrix products, block_forward(): jnp.einsum('rqhd,rkhd->rhqk', queries, row_keys, preferred_element_type=j...  31.8 us
    reduce_sum x2, other arithmetic, block_forward(): jnp.sum(jnp.exp(scores - highest), axis=-1, keepdims=True)  29.7 us
    convert_element_type x1, other arithmetic, per_device(): grad_scores = (weights * (grad_weights - inner_sum)).astype(jnp.bfloat16)  28 us
  transfers between devices with their start and end apart: 4, of which 4 were waited for; matrix products, arithmetic and copies ran while one was open for 15% of the time, Pallas kernels for 0%

commit v1 on v0

--- a/solution.py
+++ b/solution.py
@@ -8,6 +8,12 @@
 HEAD_DIM = 64
 PREFIX = 10
 best_precision = lax.Precision.HIGHEST
+
+
+def mark_slices_now(local_block, along_axis, lane_axis):
+    vec_out = lax.psum(local_block, along_axis)
+    w2 = lax.psum(vec_out, lane_axis)
+    return w2
 
 
 def layer_norm(values, norm_gain, norm_shift):
@@ -272,8 +278,8 @@
     grad_table, grad_lift, grad_liftbias, grad_fan, grad_fanbias = prefix_grads(
         prefix_grad, prefix_table, lift_weight, fan_weight, lifted, lifted_low
     )
-    grad_table, grad_lift, grad_liftbias, grad_fan, grad_fanbias = lax.psum(
-        (grad_table, grad_lift, grad_liftbias, grad_fan, grad_fanbias), ("seq", "dp")
+    grad_table, grad_lift, grad_liftbias, grad_fan, grad_fanbias = mark_slices_now(
+        (grad_table, grad_lift, grad_liftbias, grad_fan, grad_fanbias), "dp", "seq"
     )
     return (activations, input_grad, grad_table, grad_lift, grad_liftbias, grad_fan, grad_fanbias)
 

time: 674 us -> 822 us (1.22)
  waiting for transfers between devices: 207 us -> 353 us
  blocking collectives: 40.9 us -> 49.8 us
    psum x1 -> x2, waiting for transfers between devices: 43.5 us -> 189 us  [the longest x1 184 us: mark_slices_now(): vec_out = lax.psum(local_block, along_axis)]
    psum x1 -> x2, blocking collectives: 40.9 us -> 49.8 us  [the longest x1 36.1 us: mark_slices_now(): vec_out = lax.psum(local_block, along_axis)]
  transfers between devices with their start and end apart: 4 -> 5, of which waited for: 4 -> 5; matrix products, arithmetic and copies ran while one was open for 15% -> 15% of each run, Pallas kernels for 0% -> 0%
where the time goes in v1:
time: 822 us; the launch traced here: 817 us
  waiting for transfers between devices  353 us (43%)
  matrix products  237 us (29%)
  other arithmetic  81.5 us (10%)
  local copies, waits for them, and re-layouts  81.1 us (10%)
  blocking collectives  49.8 us (6%)
  between operations  14.8 us (2%)
    psum x1, waiting for transfers between devices, mark_slices_now(): vec_out = lax.psum(local_block, along_axis)  184 us
    all_gather x2, waiting for transfers between devices, block_forward(): row_keyval = lax.all_gather(local_keyval, 'seq', axis=1, tiled=True)  91.8 us
    reduce_scatter x1, waiting for transfers between devices, per_device(): lax.psum_scatter(jnp.concatenate([grad_keys.reshape(tok_count * lax.axis_...  71.7 us
    psum x1, blocking collectives, mark_slices_now(): vec_out = lax.psum(local_block, along_axis)  36.1 us
    dot_general x2, matrix products, block_forward(): jnp.einsum('rhqk,rkhd->rqhd', rounded, row_values, preferred_element_type...  34.5 us
    dot_general x2, matrix products, block_forward(): jnp.einsum('rqhd,rkhd->rhqk', queries, row_keys, preferred_element_type=j...  31.8 us
    reduce_sum x2, other arithmetic, block_forward(): jnp.sum(jnp.exp(scores - highest), axis=-1, keepdims=True)  29.7 us
    convert_element_type x1, other arithmetic, per_device(): grad_scores = (weights * (grad_weights - inner_sum)).astype(jnp.bfloat16)  28.4 us
  transfers between devices with their start and end apart: 5, of which 5 were waited for; matrix products, arithmetic and copies ran while one was open for 15% of the time, Pallas kernels for 0%

profile of v1, /device:TPU:0, one launch (start us, length us, event | category | flops | bytes accessed | tf_op | source)
XLA Modules:
  0.0 817.1 jit_solution(14372100279311023988)
XLA Ops:
  10.5 6.6 add_convert_fusion.1
  20.8 2.3 slice.48
  28.7 52.7 %all-gather.3.cloned.1.call-done = bf16[2,1024,2048]{2,1,0:T(8,128)(2,1)} async-done(((bf16[2,256,2048]{2,1,0:T(8,128)(2,1)}), bf16[2,1024,2048]{2,1,0:T(8,128)(2,1)}) %all-gather.3.cloned.1.call-update) | async-done | bytes 8388624 | tf_op jit(solution)/shard_map/all_gather | solution.py:54
  81.4 6.0 fusion.174
  87.4 6.2 copy.171
  93.6 6.2 copy.173
  99.8 15.9 %fusion = (f32[2,16,256]{2,1,0:T(8,128)S(1)}, f32[2,16,256,1024]{3,2,1,0:T(8,128)}) fusion(pred[2,256,1024]{2,1,0:T(8,128)(4,1)S(1)} %broadcast_and_fusion, bf16[2,256,16,64]{1,3,2,0:T(8,128)(2,1)} %bitcast.197, bf16[2,1024,16,64]{1,3,2,0:T(8,128)(2,1)} %bitcast.195), kind=kOutput, calls=%fused_computation.8 | convolution fusion | flops 1098899456 | bytes 39354368 | tf_op jit(solution)/shard_map/rqhd,rkhd->rhqk/dot_general | solution.py:61
  116.0 14.9 %exponential_reduce_fusion.1 = f32[2,16,256]{2,1,0:T(8,128)S(1)} fusion(f32[2,16,256,1024]{3,2,1,0:T(8,128)} %get-tuple-element.65, f32[2,16,256]{2,1,0:T(8,128)S(1)} %max.22, pred[2,256,1024]{2,1,0:T(8,128)(4,1)S(1)} %broadcast_and_fusion), kind=kLoop, calls=%fused_computation.6 | loop fusion | flops 33546240 | bytes 34144256 | tf_op jit(solution)/shard_map/reduce_sum | solution.py:76
  132.9 17.5 %fusion.74 = bf16[2,256,16,64]{1,3,2,0:T(8,128)(2,1)} fusion(f32[16,64,2,256]{3,1,0,2:T(8,128)} %fusion.137, bf16[2,1024,16,64]{1,3,2,0:T(8,128)(2,1)} %bitcast.198, f32[2,16,256,1024]{3,2,1,0:T(8,128)} %get-tuple-element.65, f32[2,16,256]{2,1,0:T(8,128)S(1)} %log_add_fusion.1, pred[2,256,1024]{2,1,0:T(8,128)(4,1)} %copy-done.3), kind=kOutput, calls=%fused_computation.94 | convolution fusion | flops 1108344832 | bytes 41451520 | tf_op jit(solution)/shard_map/rhqk,rkhd->rqhd/dot_general | solution.py:84
  150.5 2.7 fusion.176
  153.7 10.4 %fusion.19 = bf16[2,256,4096]{2,1,0:T(8,128)(2,1)S(1)} fusion(bf16[1024,4096]{1,0:T(8,128)(2,1)} %param.33, f32[4096]{0:T(1024)S(1)} %copy-done.46, f32[2,256,1024]{2,1,0:T(8,128)S(1)} %get-tuple-element.67, f32[1024]{0:T(1024)S(1)} %copy-done.50, f32[1024]{0:T(1024)S(1)} %copy-done.39, f32[2,256]{1,0:T(2,128)S(1)} %add_rsqrt_fusion, ...), kind=kOutput, calls=%fused_computation.30 | convolution fusion | flops 4318560256 | bytes 14708736 | tf_op jit(solution)/shard_map/dot_general | solution.py:97
  164.2 5.5 add_convert_fusion.3
  170.5 4.0 add_convert_fusion
  177.9 12.7 %fusion.20 = f32[2,256,4096]{2,1,0:T(8,128)} fusion(bf16[4096,1024]{1,0:T(8,128)(2,1)} %param.35, bf16[2,256,1024]{2,1,0:T(8,128)(2,1)} %param.22, pred[2,256]{1,0:T(4,128)(4,1)S(1)} %compare_and_fusion), kind=kOutput, calls=%fused_computation.32 | convolution fusion | flops 4295491584 | bytes 17826304 | tf_op jit(solution)/shard_map/rcd,fd->rcf/dot_general | solution.py:203
  190.6 2.3 slice.54
  192.9 2.4 copy.185
  197.0 39.1 %all-gather.5.cloned.1.call-done = bf16[2,1024,2048]{2,1,0:T(8,128)(2,1)} async-done(((bf16[2,256,2048]{2,1,0:T(8,128)(2,1)}), bf16[2,1024,2048]{2,1,0:T(8,128)(2,1)}) %all-gather.5.cloned.1.call-update) | async-done | bytes 8388624 | tf_op jit(solution)/shard_map/all_gather | solution.py:52
  236.2 6.0 fusion.173
  242.2 6.2 copy.186
  248.4 6.2 copy.184
  254.6 15.9 %fusion.1 = (f32[2,16,256]{2,1,0:T(8,128)S(1)}, f32[2,16,256,1024]{3,2,1,0:T(8,128)}) fusion(pred[2,256,1024]{2,1,0:T(8,128)(4,1)} %copy-done.3, bf16[2,256,16,64]{1,3,2,0:T(8,128)(2,1)} %bitcast.185, bf16[2,1024,16,64]{1,3,2,0:T(8,128)(2,1)} %bitcast.182), kind=kOutput, calls=%fused_computation.9 | convolution fusion | flops 1098899456 | bytes 39354368 | tf_op jit(solution)/shard_map/rqhd,rkhd->rhqk/dot_general | solution.py:61
  270.6 14.9 %exponential_reduce_fusion = f32[2,16,256]{2,1,0:T(8,128)S(1)} fusion(f32[2,16,256,1024]{3,2,1,0:T(8,128)} %get-tuple-element.69, f32[2,16,256]{2,1,0:T(8,128)S(1)} %max.23, pred[2,256,1024]{2,1,0:T(8,128)(4,1)S(1)} %copy-done.4), kind=kLoop, calls=%fused_computation.3 | loop fusion | flops 33546240 | bytes 34144256 | tf_op jit(solution)/shard_map/reduce_sum | solution.py:76
  286.2 17.0 %fusion.141 = f32[2,16,64,256]{3,2,1,0:T(8,128)} fusion(bf16[2,1024,16,64]{1,3,2,0:T(8,128)(2,1)} %bitcast.188, f32[2,16,256,1024]{3,2,1,0:T(8,128)} %get-tuple-element.69, f32[2,16,256]{2,1,0:T(8,128)S(1)} %log_add_fusion, pred[2,256,1024]{2,1,0:T(8,128)(4,1)} %copy-done.3), kind=kOutput, calls=%fused_computation.169 | convolution fusion | flops 1107296256 | bytes 40402944 | tf_op jit(solution)/shard_map/rhqk,rkhd->rqhd/dot_general | solution.py:84
  303.2 2.2 fusion.67
  309.0 23.9 %multiply_reduce_fusion.1 = (f32[2,256]{1,0:T(2,128)}, f32[2,256,1024]{2,1,0:T(8,128)}) fusion(f32[2,256,1024]{2,1,0:T(8,128)} %copy-done.8, f32[2,256]{1,0:T(2,128)S(1)} %broadcast_multiply_fusion, f32[1024]{0:T(1024)} %param.31, bf16[1024,4096]{1,0:T(8,128)(2,1)} %param.33, f32[2,256,4096]{2,1,0:T(8,128)} %fusion.20, f32[4096]{0:T(1024)} %param.34, ...), kind=kOutput, calls=%fused_computation.97 | convolution fusion | flops 8638693376 | bytes 21002240 | tf_op jit(solution)/shard_map/rcf,df->rcd/dot_general | solution.py:208
  333.7 2.9 fusion.172
  337.9 2.4 fusion.77
  344.1 27.3 %multiply_reduce_fusion = (f32[2,16,256]{2,1,0:T(8,128)}, f32[2,16,256,1024]{3,2,1,0:T(8,128)}) fusion(f32[2,16,256,1024]{3,2,1,0:T(8,128)} %get-tuple-element.69, f32[2,16,256]{2,1,0:T(8,128)S(1)} %log_add_fusion, pred[2,256,1024]{2,1,0:T(8,128)(4,1)S(1)} %copy-done.5, bf16[2,256,16,64]{1,3,2,0:T(8,128)(2,1)} %bitcast.192, ...), kind=kOutput, calls=%fused_computation.1 | convolution fusion | flops 1115676672 | bytes 72941568 | tf_op jit(solution)/shard_map/rqhd,rkhd->rhqk/dot_general | solution.py:220
  376.9 3.3 fusion.180
  380.3 4.6 fusion.152
  384.9 2.4 convolution_bitcast_fusion
  387.3 28.4 %multiply_convert_fusion = bf16[2,16,256,1024]{3,2,1,0:T(8,128)(2,1)} fusion(f32[2,16,256,1024]{3,2,1,0:T(8,128)} %get-tuple-element.75, f32[2,16,256,1024]{3,2,1,0:T(8,128)} %get-tuple-element.69, f32[2,16,256]{2,1,0:T(8,128)S(1)} %add.290, f32[2,16,256]{2,1,0:T(8,128)S(1)} %log_add_fusion, pred[2,256,1024]{2,1,0:T(8,128)(4,1)S(1)} %copy-done.5), kind=kLoop, calls=%fused_computation | loop fusion | flops 50331648 | bytes 84475904 | tf_op jit(solution)/shard_map/convert_element_type | solution.py:229
  415.8 184.3 %all-reduce.7.cloned.1.call-done = (f32[1024,512]{0,1:T(8,128)}, f32[512,2048]{1,0:T(8,128)}) async-done(((f32[1024,512]{0,1:T(8,128)}, f32[512,2048]{1,0:T(8,128)}), (f32[1024,512]{0,1:T(8,128)}, f32[512,2048]{1,0:T(8,128)})) %all-reduce.7.cloned.1.call-update) | async-done | bytes 6291472 | tf_op jit(solution)/shard_map/psum | solution.py:14
  600.2 18.3 %convolution_convert_fusion = bf16[2,16,64,1024]{3,2,1,0:T(8,128)(2,1)} fusion(bf16[2,256,16,64]{1,3,2,0:T(8,128)(2,1)} %bitcast.194, f32[2,16,256,1024]{3,2,1,0:T(8,128)} %get-tuple-element.69, f32[2,16,256]{2,1,0:T(8,128)S(1)} %log_add_fusion, pred[2,256,1024]{2,1,0:T(8,128)(4,1)S(1)} %copy-done.5), kind=kOutput, calls=%fused_computation.66 | convolution fusion | flops 1109393408 | bytes 39354368 | tf_op jit(solution)/shard_map/rhqk,rqhd->krhd/dot_general | solution.py:244
  618.5 6.3 copy.206
  624.8 10.9 %multiply_convert_fusion.1 = bf16[2,16,64,1024]{3,2,1,0:T(8,128)(2,1)} fusion(bf16[2,256,16,64]{1,3,2,0:T(8,128)(2,1)S(1)} %bitcast.187, bf16[2,16,256,1024]{3,2,1,0:T(8,128)(2,1)} %multiply_convert_fusion), kind=kOutput, calls=%fused_computation.42 | convolution fusion | flops 1077936128 | bytes 22020096 | tf_op jit(solution)/shard_map/rhqk,rqhd->krhd/dot_general | solution.py:241
  635.7 6.5 copy.205
  642.2 8.2 pad_maximum_fusion
  650.4 12.5 %fusion.181 = f32[2,16,64,256]{3,2,1,0:T(8,128)S(1)} fusion(bf16[2,1024,16,64]{1,3,2,0:T(8,128)(2,1)} %bitcast.183, bf16[2,16,256,1024]{3,2,1,0:T(8,128)(2,1)} %multiply_convert_fusion), kind=kOutput, calls=%fused_computation.225 | convolution fusion | flops 1073741824 | bytes 23068672 | tf_op jit(solution)/shard_map/rhqk,rkhd->rqhd/dot_general | solution.py:231
  666.0 2.2 fusion.182
  668.2 36.1 %all-reduce = (f32[10,1024]{1,0:T(8,128)S(1)}, f32[512]{0:T(512)S(1)}, f32[2048]{0:T(1024)S(1)}) all-reduce(f32[10,1024]{1,0:T(8,128)S(1)} %fusion.182, f32[512]{0:T(512)S(1)} %get-tuple-element.78, f32[2048]{0:T(1024)S(1)} %reduce_sum.231), channel_id=1, replica_groups=mesh['seq'=4,'dp'=8] {'dp'}, use_global_device_ids=true, to_apply=%region_23.24 | all-reduce | flops 12800 | bytes 102400 | tf_op jit(solution)/shard_map/psum | solution.py:14
  704.3 13.7 %all-reduce.2 = (f32[10,1024]{1,0:T(8,128)}, f32[512]{0:T(512)}, f32[2048]{0:T(1024)}) all-reduce(f32[10,1024]{1,0:T(8,128)S(1)} %get-tuple-element.44, f32[512]{0:T(512)S(1)} %get-tuple-element.45, f32[2048]{0:T(1024)S(1)} %get-tuple-element.46), channel_id=1, replica_groups=mesh['seq'=4,'dp'=8] {'seq'}, use_global_device_ids=true, to_apply=%region_24.25 | all-reduce | flops 12800 | bytes 102400 | tf_op jit(solution)/shard_map/psum | solution.py:15
  718.0 4.7 all-reduce.9.cloned.1.call-done
  722.6 2.9 copy.212
  725.5 71.7 %reduce-scatter.2.cloned.1.call-done = bf16[256,2,2048]{2,0,1:T(8,128)(2,1)} async-done(((bf16[1024,2,2048]{2,0,1:T(8,128)(2,1)}), bf16[256,2,2048]{2,0,1:T(8,128)(2,1)}) %reduce-scatter.2.cloned.1.call-update) | async-done | bytes 2097168 | tf_op jit(solution)/shard_map/reduce_scatter | solution.py:247
  797.3 6.5 fusion.63
  805.3 2.0 add_add_fusion.2
  808.3 2.0 copy.279
  (184 shorter events, 42.3 us)
Async XLA Ops:
  7.2 143.3 %copy-start = (bf16[1024,1024]{1,0:T(8,128)(2,1)S(1)}, bf16[1024,1024]{1,0:T(8,128)(2,1)}, u32[]{:S(2)}) copy-start(bf16[1024,1024]{1,0:T(8,128)(2,1)} %param.29) | copy-start | bytes 6291460
  7.2 74.2 %all-gather.3.cloned.1.call-start = ((), (), s32[]{:S(2)}) async-start(), calls=%async_computation.1 | async-start | bytes 10485760 | tf_op jit(solution)/shard_map/all_gather | solution.py:54
  18.7 4.3 copy-start.15
  18.7 4.3 copy-start.27
  18.7 4.3 copy-start.43
  18.7 4.6 copy-start.38
  20.3 215.9 %all-gather.5.cloned.1.call-start = ((), (), s32[]{:S(2)}) async-start(), calls=%async_computation.2 | async-start | bytes 10485760 | tf_op jit(solution)/shard_map/all_gather | solution.py:52
  23.0 4.5 copy-start.44
  25.6 169.8 %copy-start.20 = (bf16[10,16,64]{2,1,0:T(8,128)(2,1)}, bf16[10,16,64]{2,1,0:T(8,128)(2,1)S(1)}, u32[]{:S(2)}) copy-start(bf16[10,16,64]{2,1,0:T(8,128)(2,1)S(1)} %reshape.304) | copy-start | bytes 61444
  28.7 87.3 %copy-start.3 = (pred[2,256,1024]{2,1,0:T(8,128)(4,1)}, pred[2,256,1024]{2,1,0:T(8,128)(4,1)S(1)}, u32[]{:S(2)}) copy-start(pred[2,256,1024]{2,1,0:T(8,128)(4,1)S(1)} %broadcast_and_fusion) | copy-start | bytes 1572868
  99.8 15.9 %copy-start.11 = (f32[16,10,2,256]{3,1,2,0:T(8,128)S(1)}, f32[16,10,2,256]{3,1,2,0:T(8,128)}, u32[]{:S(2)}) copy-start(f32[16,10,2,256]{3,1,2,0:T(8,128)} %copy-done.10) | copy-start | bytes 983044
  132.9 17.5 %copy-start.2 = (bf16[2,256,1024]{2,1,0:T(8,128)(2,1)S(1)}, bf16[2,256,1024]{2,1,0:T(8,128)(2,1)}, u32[]{:S(2)}) copy-start(bf16[2,256,1024]{2,1,0:T(8,128)(2,1)} %param.21) | copy-start | bytes 3145732
  132.9 17.5 %copy-start.29 = (f32[1024]{0:T(1024)S(1)}, f32[1024]{0:T(1024)}, u32[]{:S(2)}) copy-start(f32[1024]{0:T(1024)} %param.30) | copy-start | bytes 12292
  150.5 3.2 copy-start.39
  150.5 3.2 copy-start.46
  150.5 3.2 copy-start.50
  150.5 13.7 %slice-start = ((s8[8388608]{0:T(1024)(128)(4,1)}), s8[4194304]{0:T(1024)(128)(4,1)S(1)}, s32[]{:S(2)}) async-start(s8[8388608]{0:T(1024)(128)(4,1)} %bitcast.206), calls=%async_computation.6 | async-start | bytes 8388608
  150.5 19.9 %slice-start.2 = ((s8[6291456]{0:T(1024)(128)(4,1)}), s8[4194304]{0:T(1024)(128)(4,1)S(1)}, s32[]{:S(2)}) async-start(s8[6291456]{0:T(1024)(128)(4,1)} %bitcast.208), calls=%async_computation.8 | async-start | bytes 8388608
  153.7 10.5 %slice-start.1 = ((s8[8388608]{0:T(1024)(128)(4,1)}), s8[4194304]{0:T(1024)(128)(4,1)S(1)}, s32[]{:S(2)}) async-start(s8[8388608]{0:T(1024)(128)(4,1)} %bitcast.206), calls=%async_computation.7 | async-start | bytes 8388608
  153.7 10.5 %copy-start.48 = (f32[1024]{0:T(1024)S(1)}, f32[1024]{0:T(1024)}, u32[]{:S(2)}) copy-start(f32[1024]{0:T(1024)} %param.36) | copy-start | bytes 12292
  153.7 16.7 %slice-start.3 = ((s8[6291456]{0:T(1024)(128)(4,1)}), s8[2097152]{0:T(1024)(128)(4,1)S(1)}, s32[]{:S(2)}) async-start(s8[6291456]{0:T(1024)(128)(4,1)} %bitcast.208), calls=%async_computation.9 | async-start | bytes 4194304
  164.2 6.3 copy-start.36
  164.2 6.3 copy-start.47
  164.2 6.2 copy-start.49
  170.0 4.5 copy-start.30
  170.4 4.1 copy-start.32
  170.5 4.0 copy-start.34
  177.7 422.4 %all-reduce.7.cloned.1.call-start = ((), (), s32[]{:S(2)}) async-start(), calls=%async_computation.4 | async-start | bytes 12582912 | tf_op jit(solution)/shard_map/psum | solution.py:14
  177.9 12.8 %copy-start.40 = (pred[2,256]{1,0:T(4,128)(4,1)}, pred[2,256]{1,0:T(4,128)(4,1)S(1)}, u32[]{:S(2)}) copy-start(pred[2,256]{1,0:T(4,128)(4,1)S(1)} %compare_and_fusion) | copy-start | bytes 1540
  254.6 16.0 %copy-start.4 = (pred[2,256,1024]{2,1,0:T(8,128)(4,1)S(1)}, pred[2,256,1024]{2,1,0:T(8,128)(4,1)}, u32[]{:S(2)}) copy-start(pred[2,256,1024]{2,1,0:T(8,128)(4,1)} %copy-done.3) | copy-start | bytes 1572868
  332.9 5.0 copy-start.22
  332.9 5.0 copy-start.41
  340.3 3.8 copy-start.5
  344.1 31.4 %copy-start.6 = (bf16[2,256,1024]{1,2,0:T(8,128)(2,1)S(1)}, bf16[2,256,1024]{1,2,0:T(8,128)(2,1)}, u32[]{:S(2)}) copy-start(bf16[2,256,1024]{1,2,0:T(8,128)(2,1)} %copy.185) | copy-start | bytes 3145732
  375.6 9.3 %copy-start.28 = (bf16[10,1024]{1,0:T(8,128)(2,1)S(1)}, bf16[10,1024]{1,0:T(8,128)(2,1)}, u32[]{:S(2)}) copy-start(bf16[10,1024]{1,0:T(8,128)(2,1)} %param.37) | copy-start | bytes 61444
  380.3 7.0 copy-start.25
  387.3 335.4 %all-reduce.9.cloned.1.call-start = ((), (), s32[]{:S(2)}) async-start(), calls=%async_computation.5 | async-start | bytes 12582912 | tf_op jit(solution)/shard_map/psum | solution.py:15
  600.1 197.1 %reduce-scatter.2.cloned.1.call-start = ((), (), s32[]{:S(2)}) async-start(), calls=%async_computation.3 | async-start | bytes 10485760 | tf_op jit(solution)/shard_map/reduce_scatter | solution.py:247
  650.4 12.5 %copy-start.19 = (bf16[2,16,256,10]{2,1,3,0:T(8,128)(2,1)S(1)}, bf16[2,16,256,10]{2,1,3,0:T(8,128)(2,1)}, u32[]{:S(2)}) copy-start(bf16[2,16,256,10]{2,1,3,0:T(8,128)(2,1)} %copy-done.18) | copy-start | bytes 491524
  650.4 12.5 %copy-start.21 = (bf16[10,16,64]{2,1,0:T(8,128)(2,1)S(1)}, bf16[10,16,64]{2,1,0:T(8,128)(2,1)}, u32[]{:S(2)}) copy-start(bf16[10,16,64]{2,1,0:T(8,128)(2,1)} %copy-done.20) | copy-start | bytes 61444
  663.0 3.0 copy-start.26
  664.4 132.8 %copy-start.31 = (f32[2,256]{1,0:T(2,128)S(1)}, f32[2,256]{1,0:T(2,128)}, u32[]{:S(2)}) copy-start(f32[2,256]{1,0:T(2,128)} %copy-done.30) | copy-start | bytes 6148
  664.5 132.8 %copy-start.37 = (f32[1024]{0:T(1024)S(1)}, f32[1024]{0:T(1024)}, u32[]{:S(2)}) copy-start(f32[1024]{0:T(1024)} %param.25) | copy-start | bytes 12292
  797.2 6.5 copy-start.33
  797.2 6.6 copy-start.35
  797.2 7.3 copy-start.23
  797.2 7.3 copy-start.42
  805.3 2.9 copy-start.14
  (12 other events, 17.6 us)
Sparse Core Ops, SparseCore 0:
  20.4 60.9 all-gather.2
  177.9 58.2 all-gather.4
  387.4 212.6 all-reduce.6
  602.5 120.0 all-reduce.8
  725.2 71.9 reduce-scatter.1
